TPU v7x, 32 devices: a whole 2x2x4 slice. The times are simulated.
32 devices in a mesh: pair: 8 (over z, y), aux: 4 (over x, core).
Axes of the slice: x: 2, y: 2, z: 4, core: 2. Of those that a mesh axis runs over, the one named last changes fastest.
Arguments:
- pair_factors: bfloat16 [16384, 16384], P('pair', 'aux'), may hold values from -0.077339804 to 0.077339804
- pair_weights: float32 [16384], P('pair'), may hold values from 0.08 to 0.8
- probes: float32 [16384, 64], P('aux'), may hold values from -12 to 12
Outputs:
- last_vectors: float32 [16384, 64], P('aux', 'pair')
- moments: float32 [9], replicated
- energy: float32 [1], replicated
All inputs are finite; a program needn't handle non-finite values.
Results may differ from a plain program's by a relative error of at most 0.019.
Values may be sent and summed in bfloat16 or wider, within the bound.
No kernel may reach another device: no remote copies, remote signals or barrier semaphores. Data moves between devices by JAX's collectives and lax.ppermute only.
A program may use at most 64 MiB of HBM per device.

v0:
```python
import jax
import jax.numpy as jnp
import numpy as np
from jax import lax
from jax.sharding import PartitionSpec as P

ITERS = 8
spread = 5.0


def cheb_coefficients(order_count):
    node_count = 64
    angles = (np.arange(node_count) + 0.5) * np.pi / node_count
    samples = np.log(1.0 + spread * (np.cos(angles) + 1.0) / 2.0)
    values = [
        2.0 / node_count * np.sum(samples * np.cos(degree * angles))
        for degree in range(order_count)
    ]
    values[0] = values[0] / 2.0
    return np.array(values)


def per_device(pair_factors, pair_weights, probes):
    probe_total = probes.shape[1]
    divisor = probe_total * probes.shape[0] * lax.axis_size("aux")
    share = probe_total // lax.axis_size("pair")
    start = lax.axis_index("pair") * share
    own_probes = lax.dynamic_slice_in_dim(probes, start, share, 1)
    partials = [jnp.sum(own_probes * own_probes)]
    previous = probes
    current = probes
    for degree in range(ITERS):
        rows = jnp.dot(
            pair_factors, current.astype(jnp.bfloat16), preferred_element_type=jnp.float32
        )
        rows = lax.psum(rows, "aux")
        scaled = (pair_weights[:, None] * rows).astype(jnp.bfloat16)
        image = lax.psum(
            lax.dot_general(
                pair_factors, scaled, (((0,), (0,)), ((), ())), preferred_element_type=jnp.float32
            ),
            "pair",
        )
        mapped = 2.0 / spread * image - current
        following = mapped if degree == 0 else 2.0 * mapped - previous
        previous, current = (current, following)
        own_share = lax.dynamic_slice_in_dim(current, start, share, 1)
        partials.append(jnp.sum(own_probes * own_share))
    own_share = lax.dynamic_slice_in_dim(current, start, share, 1)
    totals = lax.psum(jnp.stack(partials), ("pair", "aux"))
    moments = totals / divisor
    coefficients = jnp.asarray(cheb_coefficients(ITERS + 1)).astype(moments.dtype)
    energy = jnp.sum(coefficients * moments).reshape(1)
    return (own_share, moments, energy)


def solution(mesh):
    placed = (P("pair", "aux"), P("pair"), P("aux", None))
    return jax.shard_map(
        per_device,
        mesh=mesh,
        in_specs=placed,
        out_specs=(P("aux", "pair"), P(), P()),
        check_vma=False,
    )
```

profile of v0, /device:TPU:0, one launch (start us, length us, event | category | flops | bytes accessed | tf_op | source)
XLA Modules:
  0.0 1159.6 jit_solution(14180925838934480082)
XLA Ops:
  7.2 0.0 all-reduce.17.cloned.1.call-start
  7.2 11.6 fusion.7
  18.8 0.0 all-reduce.19.cloned.1.call-start
  18.8 39.1 %all-reduce.17.cloned.1.call-done = f32[2048,64]{1,0:T(8,128)} async-done(((f32[2048,64]{1,0:T(8,128)}), f32[2048,64]{1,0:T(8,128)}) %all-reduce.17.cloned.1.call-update) | async-done | bytes 524304 | tf_op jit(solution)/shard_map/psum | solution.py:36
  58.0 10.3 convolution_bitcast_fusion.7
  68.3 0.0 all-reduce.19.cloned.1.call-update
  68.3 0.0 all-reduce.21.cloned.1.call-start
  68.3 78.9 %all-reduce.19.cloned.1.call-done = f32[4096,64]{0,1:T(8,128)} async-done(((f32[4096,64]{0,1:T(8,128)}), f32[4096,64]{0,1:T(8,128)}) %all-reduce.19.cloned.1.call-update) | async-done | bytes 1048592 | tf_op jit(solution)/shard_map/psum | solution.py:38
  147.3 1.3 multiply_subtract_fusion.6
  148.6 9.2 convolution_bitcast_fusion.14
  157.8 0.6 all-reduce.23.cloned.1.call-start
  158.4 35.5 %all-reduce.21.cloned.1.call-done = f32[2048,64]{1,0:T(8,128)} async-done(((f32[2048,64]{1,0:T(8,128)}), f32[2048,64]{1,0:T(8,128)}) %all-reduce.21.cloned.1.call-update) | async-done | bytes 524304 | tf_op jit(solution)/shard_map/psum | solution.py:36
  193.8 10.3 convolution_bitcast_fusion.6
  204.1 0.0 all-reduce.25.cloned.1.call-start
  204.2 79.0 %all-reduce.23.cloned.1.call-done = f32[4096,64]{0,1:T(8,128)} async-done(((f32[4096,64]{0,1:T(8,128)}), f32[4096,64]{0,1:T(8,128)}) %all-reduce.23.cloned.1.call-update) | async-done | bytes 1048592 | tf_op jit(solution)/shard_map/psum | solution.py:38
  283.2 1.4 multiply_subtract_fusion.5
  284.6 9.2 convolution_bitcast_fusion.13
  293.8 0.0 all-reduce.27.cloned.1.call-start
  293.8 36.0 %all-reduce.25.cloned.1.call-done = f32[2048,64]{1,0:T(8,128)} async-done(((f32[2048,64]{1,0:T(8,128)}), f32[2048,64]{1,0:T(8,128)}) %all-reduce.25.cloned.1.call-update) | async-done | bytes 524304 | tf_op jit(solution)/shard_map/psum | solution.py:36
  329.8 10.3 convolution_bitcast_fusion.5
  340.1 0.0 all-reduce.29.cloned.1.call-start
  340.2 79.0 %all-reduce.27.cloned.1.call-done = f32[4096,64]{0,1:T(8,128)} async-done(((f32[4096,64]{0,1:T(8,128)}), f32[4096,64]{0,1:T(8,128)}) %all-reduce.27.cloned.1.call-update) | async-done | bytes 1048592 | tf_op jit(solution)/shard_map/psum | solution.py:38
  419.2 1.4 multiply_subtract_fusion.4
  420.6 9.2 convolution_bitcast_fusion.12
  429.8 0.2 all-reduce.31.cloned.1.call-start
  430.0 35.8 %all-reduce.29.cloned.1.call-done = f32[2048,64]{1,0:T(8,128)} async-done(((f32[2048,64]{1,0:T(8,128)}), f32[2048,64]{1,0:T(8,128)}) %all-reduce.29.cloned.1.call-update) | async-done | bytes 524304 | tf_op jit(solution)/shard_map/psum | solution.py:36
  465.8 10.3 convolution_bitcast_fusion.4
  476.1 0.0 all-reduce.33.cloned.1.call-start
  476.2 79.0 %all-reduce.31.cloned.1.call-done = f32[4096,64]{0,1:T(8,128)} async-done(((f32[4096,64]{0,1:T(8,128)}), f32[4096,64]{0,1:T(8,128)}) %all-reduce.31.cloned.1.call-update) | async-done | bytes 1048592 | tf_op jit(solution)/shard_map/psum | solution.py:38
  555.2 1.4 multiply_subtract_fusion.3
  556.6 1.0 copy-done
  557.5 9.1 convolution_bitcast_fusion.11
  566.7 0.0 all-reduce.35.cloned.1.call-start
  566.7 36.0 %all-reduce.33.cloned.1.call-done = f32[2048,64]{1,0:T(8,128)} async-done(((f32[2048,64]{1,0:T(8,128)}), f32[2048,64]{1,0:T(8,128)}) %all-reduce.33.cloned.1.call-update) | async-done | bytes 524304 | tf_op jit(solution)/shard_map/psum | solution.py:36
  602.7 10.2 convolution_bitcast_fusion.3
  613.0 0.0 all-reduce.37.cloned.1.call-start
  613.0 78.9 %all-reduce.35.cloned.1.call-done = f32[4096,64]{0,1:T(8,128)} async-done(((f32[4096,64]{0,1:T(8,128)}), f32[4096,64]{0,1:T(8,128)}) %all-reduce.35.cloned.1.call-update) | async-done | bytes 1048592 | tf_op jit(solution)/shard_map/psum | solution.py:38
  691.9 1.7 multiply_subtract_fusion.2
  693.6 1.0 copy-done.1
  694.7 9.1 convolution_bitcast_fusion.10
  703.8 0.3 all-reduce.39.cloned.1.call-start
  704.0 35.8 %all-reduce.37.cloned.1.call-done = f32[2048,64]{1,0:T(8,128)} async-done(((f32[2048,64]{1,0:T(8,128)}), f32[2048,64]{1,0:T(8,128)}) %all-reduce.37.cloned.1.call-update) | async-done | bytes 524304 | tf_op jit(solution)/shard_map/psum | solution.py:36
  739.8 10.2 convolution_bitcast_fusion.2
  750.1 0.0 all-reduce.41.cloned.1.call-start
  750.2 78.8 %all-reduce.39.cloned.1.call-done = f32[4096,64]{0,1:T(8,128)} async-done(((f32[4096,64]{0,1:T(8,128)}), f32[4096,64]{0,1:T(8,128)}) %all-reduce.39.cloned.1.call-update) | async-done | bytes 1048592 | tf_op jit(solution)/shard_map/psum | solution.py:38
  829.0 2.0 multiply_subtract_fusion.1
  831.0 1.0 copy-done.2
  832.0 9.1 convolution_bitcast_fusion.9
  841.1 0.0 all-reduce.43.cloned.1.call-start
  841.2 36.0 %all-reduce.41.cloned.1.call-done = f32[2048,64]{1,0:T(8,128)} async-done(((f32[2048,64]{1,0:T(8,128)}), f32[2048,64]{1,0:T(8,128)}) %all-reduce.41.cloned.1.call-update) | async-done | bytes 524304 | tf_op jit(solution)/shard_map/psum | solution.py:36
  877.2 10.2 convolution_bitcast_fusion.1
  887.4 0.0 all-reduce.45.cloned.1.call-start
  887.5 78.9 %all-reduce.43.cloned.1.call-done = f32[4096,64]{0,1:T(8,128)} async-done(((f32[4096,64]{0,1:T(8,128)}), f32[4096,64]{0,1:T(8,128)}) %all-reduce.43.cloned.1.call-update) | async-done | bytes 1048592 | tf_op jit(solution)/shard_map/psum | solution.py:38
  966.3 2.0 multiply_subtract_fusion
  968.4 1.0 copy-done.3
  969.4 9.1 convolution_bitcast_fusion.8
  978.5 0.3 all-reduce.47.cloned.1.call-start
  978.8 35.7 %all-reduce.45.cloned.1.call-done = f32[2048,64]{1,0:T(8,128)} async-done(((f32[2048,64]{1,0:T(8,128)}), f32[2048,64]{1,0:T(8,128)}) %all-reduce.45.cloned.1.call-update) | async-done | bytes 524304 | tf_op jit(solution)/shard_map/psum | solution.py:36
  1014.6 10.3 convolution_bitcast_fusion
  1024.9 78.9 %all-reduce.47.cloned.1.call-done = f32[4096,64]{0,1:T(8,128)} async-done(((f32[4096,64]{0,1:T(8,128)}), f32[4096,64]{0,1:T(8,128)}) %all-reduce.47.cloned.1.call-update) | async-done | bytes 1048592 | tf_op jit(solution)/shard_map/psum | solution.py:38
  1103.8 2.6 multiply_reduce_fusion
  1106.4 5.7 stack.39
  1112.1 39.5 %psum.135 = f32[9]{0:T(128)S(1)} all-reduce(f32[9]{0:T(128)S(1)} %stack.39), channel_id=1, replica_groups=mesh['pair'=8,'aux'=4] {'pair','aux'}, use_global_device_ids=true, to_apply=%region_25.0 | all-reduce | flops 9 | bytes 72 | tf_op jit(solution)/shard_map/psum | solution.py:50
  1151.7 1.1 multiply_reduce_fusion.9
  (25 shorter events, 0.3 us)
Async XLA Ops:
  7.2 50.8 %copy-start.5 = (f32[2048]{0:T(1024)S(1)}, f32[2048]{0:T(1024)}, u32[]{:S(2)}) copy-start(f32[2048]{0:T(1024)} %param.5) | copy-start | bytes 24580
  7.2 50.8 %all-reduce.17.cloned.1.call-start = ((), (), s32[]{:S(2)}) async-start(), calls=%async_computation | async-start | bytes 2097152 | tf_op jit(solution)/shard_map/psum | solution.py:36
  18.8 128.5 %copy-start.4 = (f32[4096,64]{0,1:T(8,128)S(1)}, f32[4096,64]{0,1:T(8,128)}, u32[]{:S(2)}) copy-start(f32[4096,64]{0,1:T(8,128)} %param.6) | copy-start | bytes 3145732
  18.8 128.4 %all-reduce.19.cloned.1.call-start = ((), (), s32[]{:S(2)}) async-start(), calls=%async_computation.1 | async-start | bytes 2097152 | tf_op jit(solution)/shard_map/psum | solution.py:38
  68.3 125.5 %all-reduce.21.cloned.1.call-start = ((), (), s32[]{:S(2)}) async-start(), calls=%async_computation.2 | async-start | bytes 2097152 | tf_op jit(solution)/shard_map/psum | solution.py:36
  157.8 125.4 %all-reduce.23.cloned.1.call-start = ((), (), s32[]{:S(2)}) async-start(), calls=%async_computation.3 | async-start | bytes 2097152 | tf_op jit(solution)/shard_map/psum | solution.py:38
  204.1 125.7 %all-reduce.25.cloned.1.call-start = ((), (), s32[]{:S(2)}) async-start(), calls=%async_computation.4 | async-start | bytes 2097152 | tf_op jit(solution)/shard_map/psum | solution.py:36
  293.8 125.4 %all-reduce.27.cloned.1.call-start = ((), (), s32[]{:S(2)}) async-start(), calls=%async_computation.5 | async-start | bytes 2097152 | tf_op jit(solution)/shard_map/psum | solution.py:38
  340.1 125.7 %all-reduce.29.cloned.1.call-start = ((), (), s32[]{:S(2)}) async-start(), calls=%async_computation.6 | async-start | bytes 2097152 | tf_op jit(solution)/shard_map/psum | solution.py:36
  429.8 125.4 %all-reduce.31.cloned.1.call-start = ((), (), s32[]{:S(2)}) async-start(), calls=%async_computation.7 | async-start | bytes 2097152 | tf_op jit(solution)/shard_map/psum | solution.py:38
  476.1 126.6 %all-reduce.33.cloned.1.call-start = ((), (), s32[]{:S(2)}) async-start(), calls=%async_computation.8 | async-start | bytes 2097152 | tf_op jit(solution)/shard_map/psum | solution.py:36
  556.6 1.0 copy-start
  566.7 125.2 %all-reduce.35.cloned.1.call-start = ((), (), s32[]{:S(2)}) async-start(), calls=%async_computation.9 | async-start | bytes 2097152 | tf_op jit(solution)/shard_map/psum | solution.py:38
  613.0 126.8 %all-reduce.37.cloned.1.call-start = ((), (), s32[]{:S(2)}) async-start(), calls=%async_computation.10 | async-start | bytes 2097152 | tf_op jit(solution)/shard_map/psum | solution.py:36
  693.6 1.0 copy-start.1
  703.8 125.2 %all-reduce.39.cloned.1.call-start = ((), (), s32[]{:S(2)}) async-start(), calls=%async_computation.11 | async-start | bytes 2097152 | tf_op jit(solution)/shard_map/psum | solution.py:38
  750.1 127.0 %all-reduce.41.cloned.1.call-start = ((), (), s32[]{:S(2)}) async-start(), calls=%async_computation.12 | async-start | bytes 2097152 | tf_op jit(solution)/shard_map/psum | solution.py:36
  831.0 1.0 copy-start.2
  841.1 125.2 %all-reduce.43.cloned.1.call-start = ((), (), s32[]{:S(2)}) async-start(), calls=%async_computation.13 | async-start | bytes 2097152 | tf_op jit(solution)/shard_map/psum | solution.py:38
  887.4 127.1 %all-reduce.45.cloned.1.call-start = ((), (), s32[]{:S(2)}) async-start(), calls=%async_computation.14 | async-start | bytes 2097152 | tf_op jit(solution)/shard_map/psum | solution.py:36
  968.4 1.0 copy-start.3
  978.5 173.2 %copy-start.6 = (f32[9]{0:T(128)S(1)}, f32[9]{0:T(128)}, u32[]{:S(2)}) copy-start(f32[9]{0:T(128)} %constant.23.clone) | copy-start | bytes 112
  978.5 125.3 %all-reduce.47.cloned.1.call-start = ((), (), s32[]{:S(2)}) async-start(), calls=%async_computation.15 | async-start | bytes 2097152 | tf_op jit(solution)/shard_map/psum | solution.py:38
Sparse Core Ops, SparseCore 0:
  18.9 39.0 all-reduce.16
  68.4 78.7 all-reduce.18
  157.9 35.8 all-reduce.20
  204.3 78.8 all-reduce.22
  293.9 35.8 all-reduce.24
  340.3 78.8 all-reduce.26
  429.9 35.8 all-reduce.28
  476.2 78.8 all-reduce.30
  566.8 35.8 all-reduce.32
  613.1 78.7 all-reduce.34
  703.9 35.8 all-reduce.36
  750.2 78.7 all-reduce.38
  841.2 35.8 all-reduce.40
  887.5 78.7 all-reduce.42
  978.6 35.8 all-reduce.44
  1025.0 78.7 all-reduce.46
where the time goes:
time: 1170 us; the launch traced here: 1160 us
  waiting for transfers between devices  922 us (79%)
  matrix products  158 us (14%)
  blocking collectives  39.5 us (3%)
  other arithmetic  15.1 us (1%)
  between operations  14.3 us (1%)
    psum x8, waiting for transfers between devices, per_device(): lax.psum(lax.dot_general(pair_factors, scaled, (((0,), (0,)), ((), ())),...  631 us
    psum x8, waiting for transfers between devices, per_device(): rows = lax.psum(rows, 'aux')  290 us
    dot_general x8, matrix products, per_device(): lax.dot_general(pair_factors, scaled, (((0,), (0,)), ((), ())), preferred...  82.2 us
    dot_general x8, matrix products, per_device(): jnp.dot(pair_factors, current.astype(jnp.bfloat16), preferred_element_typ...  75.4 us
    psum x1, blocking collectives, per_device(): totals = lax.psum(jnp.stack(partials), ('pair', 'aux'))  39.5 us
  transfers between devices with their start and end apart: 16, of which 16 were waited for; matrix products, arithmetic and copies ran while one was open for 0% of the time, Pallas kernels for 0%

commit v1 on v0

--- a/solution.py
+++ b/solution.py
@@ -1,3 +1,4 @@
+import functools
 import jax
 import jax.numpy as jnp
 import numpy as np
@@ -6,6 +7,14 @@
 
 ITERS = 8
 spread = 5.0
+
+
+def treat_the_regions(original, lane_axis):
+    current_arr = lax.all_gather(original, lane_axis)
+    return jnp.sum(current_arr, 0)
+
+
+yards_check = functools.partial(treat_the_regions, lane_axis="pair")
 
 
 def cheb_coefficients(order_count):
@@ -35,11 +44,10 @@
         )
         rows = lax.psum(rows, "aux")
         scaled = (pair_weights[:, None] * rows).astype(jnp.bfloat16)
-        image = lax.psum(
+        image = yards_check(
             lax.dot_general(
                 pair_factors, scaled, (((0,), (0,)), ((), ())), preferred_element_type=jnp.float32
-            ),
-            "pair",
+            )
         )
         mapped = 2.0 / spread * image - current
         following = mapped if degree == 0 else 2.0 * mapped - previous

time: 1170 us -> 1600 us (1.37)
  waiting for transfers between devices: 922 us -> 1280 us
  local copies, waits for them, and re-layouts: 9.66 us -> 75 us
    all_gather x0 -> x8, waiting for transfers between devices: none -> 1000 us  [treat_the_regions(): current_arr = lax.all_gather(original, lane_axis)]
    psum x8 -> x0, waiting for transfers between devices: 631 us -> none  [per_device(): lax.psum(lax.dot_general(pair_factors, scaled, (((0,), (0,)), ((), ())),...]
    unnamed x14 -> x32, local copies, waits for them, and re-layouts: 3.97 us -> 69.3 us
where the time goes in v1:
time: 1600 us; the launch traced here: 1590 us
  waiting for transfers between devices  1280 us (80%)
  matrix products  158 us (10%)
  local copies, waits for them, and re-layouts  75 us (5%)
  blocking collectives  38.3 us (2%)
  other arithmetic  21.1 us (1%)
    all_gather x8, waiting for transfers between devices, treat_the_regions(): current_arr = lax.all_gather(original, lane_axis)  1000 us
    psum x8, waiting for transfers between devices, per_device(): rows = lax.psum(rows, 'aux')  279 us
    dot_general x8, matrix products, per_device(): lax.dot_general(pair_factors, scaled, (((0,), (0,)), ((), ())), preferred...  82.4 us
    dot_general x8, matrix products, per_device(): jnp.dot(pair_factors, current.astype(jnp.bfloat16), preferred_element_typ...  75.6 us
    unnamed x32, local copies, waits for them, and re-layouts  69.3 us
    psum x1, blocking collectives, per_device(): totals = lax.psum(jnp.stack(partials), ('pair', 'aux'))  38.3 us
  transfers between devices with their start and end apart: 16, of which 16 were waited for; matrix products, arithmetic and copies ran while one was open for 0% of the time, Pallas kernels for 0%

profile of v1, /device:TPU:0, one launch (start us, length us, event | category | flops | bytes accessed | tf_op | source)
XLA Modules:
  0.0 1589.3 jit_solution(4025910925350474887)
XLA Ops:
  7.2 11.6 fusion.7
  18.8 39.1 %all-reduce.9.cloned.1.call-done = f32[2048,64]{1,0:T(8,128)} async-done(((f32[2048,64]{1,0:T(8,128)}), f32[2048,64]{1,0:T(8,128)}) %all-reduce.9.cloned.1.call-update) | async-done | bytes 524304 | tf_op jit(solution)/shard_map/psum | solution.py:45
  58.0 10.3 convolution_bitcast_fusion.7
  68.6 124.9 %all-gather.17.cloned.1.call-done = f32[32768,64]{0,1:T(8,128)} async-done(((f32[4096,64]{0,1:T(8,128)}), f32[32768,64]{0,1:T(8,128)}) %all-gather.17.cloned.1.call-update) | async-done | bytes 8388624 | tf_op jit(solution)/shard_map/all_gather | solution.py:13
  193.4 8.1 copy.7
  201.5 2.1 bitcast_reduce_fusion.7
  203.8 9.2 convolution_bitcast_fusion.14
  213.0 34.6 %all-reduce.11.cloned.1.call-done = f32[2048,64]{1,0:T(8,128)} async-done(((f32[2048,64]{1,0:T(8,128)}), f32[2048,64]{1,0:T(8,128)}) %all-reduce.11.cloned.1.call-update) | async-done | bytes 524304 | tf_op jit(solution)/shard_map/psum | solution.py:45
  247.6 10.3 convolution_bitcast_fusion.6
  257.9 0.3 all-reduce.13.cloned.1.call-start
  258.2 124.8 %all-gather.19.cloned.1.call-done = f32[32768,64]{0,1:T(8,128)} async-done(((f32[4096,64]{0,1:T(8,128)}), f32[32768,64]{0,1:T(8,128)}) %all-gather.19.cloned.1.call-update) | async-done | bytes 8388624 | tf_op jit(solution)/shard_map/all_gather | solution.py:13
  383.0 8.1 copy.8
  391.1 2.0 bitcast_reduce_fusion.6
  393.1 0.2 multiply_subtract_fusion.5
  393.4 9.1 convolution_bitcast_fusion.13
  402.5 0.4 all-gather.21.cloned.1.call-start
  403.0 34.2 %all-reduce.13.cloned.1.call-done = f32[2048,64]{1,0:T(8,128)} async-done(((f32[2048,64]{1,0:T(8,128)}), f32[2048,64]{1,0:T(8,128)}) %all-reduce.13.cloned.1.call-update) | async-done | bytes 524304 | tf_op jit(solution)/shard_map/psum | solution.py:45
  437.2 10.3 convolution_bitcast_fusion.5
  447.6 125.0 %all-gather.21.cloned.1.call-done = f32[32768,64]{0,1:T(8,128)} async-done(((f32[4096,64]{0,1:T(8,128)}), f32[32768,64]{0,1:T(8,128)}) %all-gather.21.cloned.1.call-update) | async-done | bytes 8388624 | tf_op jit(solution)/shard_map/all_gather | solution.py:13
  572.6 8.1 copy.9
  580.7 2.0 bitcast_reduce_fusion.5
  582.7 0.2 multiply_subtract_fusion.4
  583.0 9.1 convolution_bitcast_fusion.12
  592.4 34.4 %all-reduce.15.cloned.1.call-done = f32[2048,64]{1,0:T(8,128)} async-done(((f32[2048,64]{1,0:T(8,128)}), f32[2048,64]{1,0:T(8,128)}) %all-reduce.15.cloned.1.call-update) | async-done | bytes 524304 | tf_op jit(solution)/shard_map/psum | solution.py:45
  626.8 10.3 convolution_bitcast_fusion.4
  637.2 125.0 %all-gather.23.cloned.1.call-done = f32[32768,64]{0,1:T(8,128)} async-done(((f32[4096,64]{0,1:T(8,128)}), f32[32768,64]{0,1:T(8,128)}) %all-gather.23.cloned.1.call-update) | async-done | bytes 8388624 | tf_op jit(solution)/shard_map/all_gather | solution.py:13
  762.2 8.1 copy.10
  770.3 2.0 bitcast_reduce_fusion.4
  772.6 1.1 copy-done
  773.6 9.2 convolution_bitcast_fusion.11
  782.8 0.4 all-gather.25.cloned.1.call-start
  783.2 34.2 %all-reduce.17.cloned.1.call-done = f32[2048,64]{1,0:T(8,128)} async-done(((f32[2048,64]{1,0:T(8,128)}), f32[2048,64]{1,0:T(8,128)}) %all-reduce.17.cloned.1.call-update) | async-done | bytes 524304 | tf_op jit(solution)/shard_map/psum | solution.py:45
  817.4 10.2 convolution_bitcast_fusion.3
  827.7 125.0 %all-gather.25.cloned.1.call-done = f32[32768,64]{0,1:T(8,128)} async-done(((f32[4096,64]{0,1:T(8,128)}), f32[32768,64]{0,1:T(8,128)}) %all-gather.25.cloned.1.call-update) | async-done | bytes 8388624 | tf_op jit(solution)/shard_map/all_gather | solution.py:13
  952.8 8.2 copy.11
  961.0 2.0 bitcast_reduce_fusion.3
  963.0 0.3 multiply_subtract_fusion.2
  963.2 1.0 copy-done.3
  964.2 9.2 convolution_bitcast_fusion.10
  973.6 34.4 %all-reduce.19.cloned.1.call-done = f32[2048,64]{1,0:T(8,128)} async-done(((f32[2048,64]{1,0:T(8,128)}), f32[2048,64]{1,0:T(8,128)}) %all-reduce.19.cloned.1.call-update) | async-done | bytes 524304 | tf_op jit(solution)/shard_map/psum | solution.py:45
  1008.0 10.2 convolution_bitcast_fusion.2
  1018.3 125.0 %all-gather.27.cloned.1.call-done = f32[32768,64]{0,1:T(8,128)} async-done(((f32[4096,64]{0,1:T(8,128)}), f32[32768,64]{0,1:T(8,128)}) %all-gather.27.cloned.1.call-update) | async-done | bytes 8388624 | tf_op jit(solution)/shard_map/all_gather | solution.py:13
  1143.3 8.3 copy.12
  1151.6 2.0 bitcast_reduce_fusion.2
  1153.8 1.0 copy-done.6
  1154.8 9.1 convolution_bitcast_fusion.9
  1163.9 0.3 all-gather.29.cloned.1.call-start
  1164.2 34.4 %all-reduce.21.cloned.1.call-done = f32[2048,64]{1,0:T(8,128)} async-done(((f32[2048,64]{1,0:T(8,128)}), f32[2048,64]{1,0:T(8,128)}) %all-reduce.21.cloned.1.call-update) | async-done | bytes 524304 | tf_op jit(solution)/shard_map/psum | solution.py:45
  1198.5 10.2 convolution_bitcast_fusion.1
  1208.9 125.0 %all-gather.29.cloned.1.call-done = f32[32768,64]{0,1:T(8,128)} async-done(((f32[4096,64]{0,1:T(8,128)}), f32[32768,64]{0,1:T(8,128)}) %all-gather.29.cloned.1.call-update) | async-done | bytes 8388624 | tf_op jit(solution)/shard_map/all_gather | solution.py:13
  1333.9 8.3 copy.13
  1342.2 2.0 bitcast_reduce_fusion.1
  1344.4 1.0 copy-done.8
  1345.3 9.1 convolution_bitcast_fusion.8
  1354.5 0.3 all-gather.31.cloned.1.call-start
  1354.8 34.3 %all-reduce.23.cloned.1.call-done = f32[2048,64]{1,0:T(8,128)} async-done(((f32[2048,64]{1,0:T(8,128)}), f32[2048,64]{1,0:T(8,128)}) %all-reduce.23.cloned.1.call-update) | async-done | bytes 524304 | tf_op jit(solution)/shard_map/psum | solution.py:45
  1389.1 10.3 convolution_bitcast_fusion
  1399.5 125.1 %all-gather.31.cloned.1.call-done = f32[32768,64]{0,1:T(8,128)} async-done(((f32[4096,64]{0,1:T(8,128)}), f32[32768,64]{0,1:T(8,128)}) %all-gather.31.cloned.1.call-update) | async-done | bytes 8388624 | tf_op jit(solution)/shard_map/all_gather | solution.py:13
  1524.5 8.1 copy.14
  1532.7 2.0 bitcast_reduce_fusion
  1534.6 2.6 multiply_reduce_fusion
  1537.2 5.7 stack.39
  1542.9 38.3 %psum.71 = f32[9]{0:T(128)S(1)} all-reduce(f32[9]{0:T(128)S(1)} %stack.39), channel_id=1, replica_groups=mesh['pair'=8,'aux'=4] {'pair','aux'}, use_global_device_ids=true, to_apply=%region_25.0 | all-reduce | flops 9 | bytes 72 | tf_op jit(solution)/shard_map/psum | solution.py:58
  1581.2 1.1 multiply_reduce_fusion.9
  (51 shorter events, 2.0 us)
Async XLA Ops:
  7.2 50.8 %copy-start.10 = (f32[2048]{0:T(1024)S(1)}, f32[2048]{0:T(1024)}, u32[]{:S(2)}) copy-start(f32[2048]{0:T(1024)} %param.5) | copy-start | bytes 24580
  7.2 50.8 %all-reduce.9.cloned.1.call-start = ((), (), s32[]{:S(2)}) async-start(), calls=%async_computation | async-start | bytes 2097152 | tf_op jit(solution)/shard_map/psum | solution.py:45
  18.8 174.6 %all-gather.17.cloned.1.call-start = ((), (), s32[]{:S(2)}) async-start(), calls=%async_computation.8 | async-start | bytes 9437184 | tf_op jit(solution)/shard_map/all_gather | solution.py:13
  68.3 135.3 %copy-start.9 = (f32[4096,64]{0,1:T(8,128)S(1)}, f32[4096,64]{0,1:T(8,128)}, u32[]{:S(2)}) copy-start(f32[4096,64]{0,1:T(8,128)} %param.6) | copy-start | bytes 3145732
  68.3 179.2 %all-reduce.11.cloned.1.call-start = ((), (), s32[]{:S(2)}) async-start(), calls=%async_computation.1 | async-start | bytes 2097152 | tf_op jit(solution)/shard_map/psum | solution.py:45
  213.0 170.1 %all-gather.19.cloned.1.call-start = ((), (), s32[]{:S(2)}) async-start(), calls=%async_computation.9 | async-start | bytes 9437184 | tf_op jit(solution)/shard_map/all_gather | solution.py:13
  257.9 179.2 %all-reduce.13.cloned.1.call-start = ((), (), s32[]{:S(2)}) async-start(), calls=%async_computation.2 | async-start | bytes 2097152 | tf_op jit(solution)/shard_map/psum | solution.py:45
  402.5 170.1 %all-gather.21.cloned.1.call-start = ((), (), s32[]{:S(2)}) async-start(), calls=%async_computation.10 | async-start | bytes 9437184 | tf_op jit(solution)/shard_map/all_gather | solution.py:13
  447.5 179.2 %all-reduce.15.cloned.1.call-start = ((), (), s32[]{:S(2)}) async-start(), calls=%async_computation.3 | async-start | bytes 2097152 | tf_op jit(solution)/shard_map/psum | solution.py:45
  592.1 170.1 %all-gather.23.cloned.1.call-start = ((), (), s32[]{:S(2)}) async-start(), calls=%async_computation.11 | async-start | bytes 9437184 | tf_op jit(solution)/shard_map/all_gather | solution.py:13
  637.1 180.3 %all-reduce.17.cloned.1.call-start = ((), (), s32[]{:S(2)}) async-start(), calls=%async_computation.4 | async-start | bytes 2097152 | tf_op jit(solution)/shard_map/psum | solution.py:45
  772.5 1.1 copy-start
  782.8 170.0 %all-gather.25.cloned.1.call-start = ((), (), s32[]{:S(2)}) async-start(), calls=%async_computation.12 | async-start | bytes 9437184 | tf_op jit(solution)/shard_map/all_gather | solution.py:13
  827.7 180.3 %all-reduce.19.cloned.1.call-start = ((), (), s32[]{:S(2)}) async-start(), calls=%async_computation.5 | async-start | bytes 2097152 | tf_op jit(solution)/shard_map/psum | solution.py:45
  952.8 10.2 copy-start.1
  963.2 1.0 copy-start.3
  973.4 170.0 %all-gather.27.cloned.1.call-start = ((), (), s32[]{:S(2)}) async-start(), calls=%async_computation.13 | async-start | bytes 9437184 | tf_op jit(solution)/shard_map/all_gather | solution.py:13
  1018.2 180.3 %all-reduce.21.cloned.1.call-start = ((), (), s32[]{:S(2)}) async-start(), calls=%async_computation.6 | async-start | bytes 2097152 | tf_op jit(solution)/shard_map/psum | solution.py:45
  1143.3 10.3 copy-start.2
  1143.3 10.3 copy-start.4
  1153.8 1.0 copy-start.6
  1163.9 170.0 %all-gather.29.cloned.1.call-start = ((), (), s32[]{:S(2)}) async-start(), calls=%async_computation.14 | async-start | bytes 9437184 | tf_op jit(solution)/shard_map/all_gather | solution.py:13
  1208.8 180.3 %all-reduce.23.cloned.1.call-start = ((), (), s32[]{:S(2)}) async-start(), calls=%async_computation.7 | async-start | bytes 2097152 | tf_op jit(solution)/shard_map/psum | solution.py:45
  1333.9 10.3 copy-start.5
  1333.9 10.3 copy-start.7
  1344.4 1.0 copy-start.8
  1354.5 170.0 %all-gather.31.cloned.1.call-start = ((), (), s32[]{:S(2)}) async-start(), calls=%async_computation.15 | async-start | bytes 9437184 | tf_op jit(solution)/shard_map/all_gather | solution.py:13
  1399.4 181.8 %copy-start.11 = (f32[9]{0:T(128)S(1)}, f32[9]{0:T(128)}, u32[]{:S(2)}) copy-start(f32[9]{0:T(128)} %constant.23.clone) | copy-start | bytes 112
Sparse Core Ops, SparseCore 0:
  18.9 39.0 all-reduce.8
  68.5 124.9 all-gather.16
  213.1 34.4 all-reduce.10
  258.1 124.9 all-gather.18
  402.7 34.4 all-reduce.12
  447.6 124.9 all-gather.20
  592.3 34.4 all-reduce.14
  637.2 124.9 all-gather.22
  782.9 34.4 all-reduce.16
  827.8 124.9 all-gather.24
  973.5 34.4 all-reduce.18
  1018.4 124.9 all-gather.26
  1164.1 34.4 all-reduce.20
  1208.9 124.9 all-gather.28
  1354.6 34.4 all-reduce.22
  1399.6 124.9 all-gather.30
